TPU v7x, 32 devices: a whole 2x2x4 slice. The times are simulated.
32 devices in a mesh: row: 8 (over z, y), col: 2 (over core), layer: 2 (over x).
Axes of the slice: x: 2, y: 2, z: 4, core: 2. Of those that a mesh axis runs over, the one named last changes fastest.
Arguments:
- matrix: float32 [1, 8, 256, 4, 2, 256], P(None, 'row', None, None, 'col'), may hold values from -8 to 113.137085, as said below
Outputs:
- factored: float32 [1, 8, 256, 4, 2, 256], P(None, 'row', None, 'layer', 'col')
Inputs may be any that keep to these rules, and one draw needn't show every extreme that they name: `matrix`: viewed as in the first step it is symmetric, its leading 2 * 256 x 2 * 256 block is positive definite, and its diagonal entries lie between 2.5 and 5 times the square root of 512.
All inputs are finite; a program needn't handle non-finite values.
Results may differ from a plain program's by a relative error of at most 0.000059.
Values sent between devices are 32-bit elements; how exact they have to be, the bound alone decides.
No kernel may reach another device: no remote copies, remote signals or barrier semaphores. Data moves between devices by JAX's collectives and lax.ppermute only.
A program may use at most 128 MiB of HBM per device.

v0:
```python
import jax
import jax.numpy as jnp
from jax import lax
from jax.sharding import PartitionSpec as P

HIGH = lax.Precision.HIGHEST


def from_root(shard, axis, root):
    mine = lax.axis_index(axis) == root
    return lax.psum(jnp.where(mine, shard, jnp.zeros_like(shard)), axis)


def factor_block(diag_block):
    lower_fac = jnp.linalg.cholesky(diag_block)
    identity = jnp.eye(diag_block.shape[0], dtype=jnp.float32)
    inverse = lax.linalg.triangular_solve(lower_fac, identity, left_side=True, lower=True)
    return (lower_fac, inverse)


def on_device(matrix):
    row_total = lax.axis_size("row")
    col_total = lax.axis_size("col")
    layer_total = lax.axis_size("layer")
    grid_row = lax.axis_index("row")
    grid_col = lax.axis_index("col")
    grid_layer = lax.axis_index("layer")
    row_blocks = matrix.shape[0]
    block_size = matrix.shape[2]
    col_blocks = matrix.shape[3]
    half = block_size // layer_total
    owned = col_blocks // layer_total
    rows = row_blocks * block_size
    tile = matrix.reshape(rows, col_blocks * block_size)
    row_ids = jnp.arange(rows) // block_size * row_total + grid_row
    column = tile[:, :block_size]
    pending = None
    total = None
    panels = []
    for section in range(2):
        diag_block = from_root(column, "row", section % row_total)
        lower_fac, inverse = factor_block(diag_block)
        solved = jnp.dot(column, inverse.T, precision=HIGH, preferred_element_type=jnp.float32)
        repeated = jnp.tile(lower_fac, (row_blocks, 1))
        complete = jnp.where(
            row_ids[:, None] > section,
            solved,
            jnp.where(row_ids[:, None] == section, repeated, 0.0),
        )
        panels.append(complete)
        share = lax.dynamic_slice_in_dim(complete, grid_layer * half, half, 1)
        share = from_root(share, "col", section % col_total)
        gathered = lax.all_gather(
            share.reshape(row_blocks, 1, block_size, half), "row", axis=1, tiled=True
        )
        grouped = gathered.reshape(col_blocks, col_total, block_size, half)
        picked = lax.dynamic_index_in_dim(grouped, grid_col, 1, keepdims=False).reshape(
            col_blocks * block_size, half
        )
        update = lax.dot_general(
            share,
            picked,
            (((1,), (1,)), ((), ())),
            precision=HIGH,
            preferred_element_type=jnp.float32,
        )
        if section == 0:
            head = lax.psum(update[:, :block_size], "layer")
            column = tile[:, :block_size] - head
            pending = update
        else:
            total = pending + update
    reduced = lax.psum_scatter(
        total.reshape(rows, col_blocks, block_size), "layer", scatter_dimension=1, tiled=True
    )
    own_part = (
        lax.dynamic_slice_in_dim(
            tile.reshape(rows, col_blocks, block_size), grid_layer * owned, owned, 1
        )
        - reduced
    )
    replacement = jnp.where(grid_col == 0, panels[0], panels[1])
    global_ids = (grid_layer * owned + jnp.arange(owned)) * col_total + grid_col
    result = jnp.where((global_ids < 2)[None, :, None], replacement[:, None, :], own_part)
    return result.reshape(row_blocks, 1, block_size, owned, 1, block_size)


def solution(mesh):
    in_specs = (P(None, "row", None, None, "col", None),)
    out_specs = P(None, "row", None, "layer", "col", None)
    return jax.shard_map(
        on_device, mesh=mesh, in_specs=in_specs, out_specs=out_specs, check_vma=False
    )
```

profile of v0, /device:TPU:0, one launch (start us, length us, event | category | flops | bytes accessed | tf_op | source)
XLA Modules:
  0.0 472.5 jit_solution(6674159370767984335)
XLA Ops:
  6.5 2.3 copy.16
  9.8 74.7 %all-reduce.7.cloned.1.call-done = f32[256,256]{0,1:T(8,128)} async-done(((f32[256,256]{0,1:T(8,128)}), f32[256,256]{0,1:T(8,128)}) %all-reduce.7.cloned.1.call-update) | async-done | bytes 262160 | tf_op jit(solution)/shard_map/psum | solution.py:11
  85.7 11.7 %cholesky.130 = f32[128,128]{1,0:T(8,128)S(1)} custom-call(f32[128,128]{1,0:T(8,128)S(1)} %cholesky.194), custom_call_target="Cholesky" | custom-call | tf_op jit(solution)/shard_map/jit(cholesky)/cholesky | solution.py:15
  97.4 9.8 %custom-call.13 = f32[1,128,128]{1,2,0:T(8,128)S(1)} custom-call(f32[1,128,128]{2,1,0:T(8,128)S(1)} %get-tuple-element.62), custom_call_target="InvertDiagBlocksLowerTriangular" | custom-call | tf_op jit(solution)/shard_map/jit(cholesky)/cholesky | solution.py:15
  107.7 11.7 %cholesky.147 = f32[128,128]{1,0:T(8,128)S(1)} custom-call(f32[128,128]{1,0:T(8,128)S(1)} %convolution_subtract_fusion.3), custom_call_target="Cholesky" | custom-call | tf_op jit(solution)/shard_map/jit(cholesky)/cholesky | solution.py:15
  122.0 4.8 %while.4 = (s32[]{:T(128)}, f32[256,256]{0,1:T(8,128)S(1)}, s32[2,2]{1,0:T(2,128)S(1)}, f32[2,128,128]{2,1,0:T(8,128)S(1)}, s32[]{:T(128)}) while((s32[]{:T(128)}, f32[256,256]{0,1:T(8,128)S(1)}, s32[2,2]{1,0:T(2,128)S(1)}, f32[2,128,128]{2,1,0:T(8,128)S(1)}, s32[]{:T(128)}) %tuple.46), condition=%wide.while_cond, body=%wide.while_body.sunk | while | flops 2 | bytes 393321 | solution.py:17
  126.8 19.7 %custom-call.14 = f32[2,128,128]{1,2,0:T(8,128)S(1)} custom-call(f32[2,128,128]{2,1,0:T(8,128)S(1)} %get-tuple-element.21), custom_call_target="InvertDiagBlocksLowerTriangular" | custom-call | tf_op jit(solution)/shard_map/triangular_solve/custom-call.0 | solution.py:17
  148.6 17.2 %all-reduce.9.cloned.1.call-done = f32[256,128]{0,1:T(8,128)} async-done(((f32[256,128]{0,1:T(8,128)}), f32[256,128]{0,1:T(8,128)}) %all-reduce.9.cloned.1.call-update) | async-done | bytes 131088 | tf_op jit(solution)/shard_map/psum | solution.py:11
  165.9 42.6 %all-gather.5.cloned.1.call-done = f32[2048,128]{0,1:T(8,128)} async-done(((f32[256,128]{0,1:T(8,128)}), f32[2048,128]{0,1:T(8,128)}) %all-gather.5.cloned.1.call-update) | async-done | bytes 1048592 | tf_op jit(solution)/shard_map/all_gather | solution.py:53
  208.5 2.1 reshape.86
  210.6 1.6 dynamic-slice_reduce_fusion.1
  215.1 22.4 %all-reduce.11.cloned.1.call-done = f32[256,256]{0,1:T(8,128)} async-done(((f32[256,256]{0,1:T(8,128)}), f32[256,256]{0,1:T(8,128)}) %all-reduce.11.cloned.1.call-update) | async-done | bytes 262160 | tf_op jit(solution)/shard_map/psum | solution.py:68
  237.5 1.7 broadcast_select_fusion
  239.5 72.3 %all-reduce.13.cloned.1.call-done = f32[256,256]{0,1:T(8,128)} async-done(((f32[256,256]{0,1:T(8,128)}), f32[256,256]{0,1:T(8,128)}) %all-reduce.13.cloned.1.call-update) | async-done | bytes 262160 | tf_op jit(solution)/shard_map/psum | solution.py:11
  313.0 11.7 %cholesky.164 = f32[128,128]{1,0:T(8,128)S(1)} custom-call(f32[128,128]{1,0:T(8,128)S(1)} %cholesky.197), custom_call_target="Cholesky" | custom-call | tf_op jit(solution)/shard_map/jit(cholesky)/cholesky | solution.py:15
  324.8 9.8 %custom-call.15 = f32[1,128,128]{1,2,0:T(8,128)S(1)} custom-call(f32[1,128,128]{2,1,0:T(8,128)S(1)} %get-tuple-element.60), custom_call_target="InvertDiagBlocksLowerTriangular" | custom-call | tf_op jit(solution)/shard_map/jit(cholesky)/cholesky | solution.py:15
  335.1 11.7 %cholesky.181 = f32[128,128]{1,0:T(8,128)S(1)} custom-call(f32[128,128]{1,0:T(8,128)S(1)} %convolution_subtract_fusion.2), custom_call_target="Cholesky" | custom-call | tf_op jit(solution)/shard_map/jit(cholesky)/cholesky | solution.py:15
  349.8 4.4 while.5
  354.2 19.7 %custom-call.16 = f32[2,128,128]{1,2,0:T(8,128)S(1)} custom-call(f32[2,128,128]{2,1,0:T(8,128)S(1)} %get-tuple-element.22), custom_call_target="InvertDiagBlocksLowerTriangular" | custom-call | tf_op jit(solution)/shard_map/triangular_solve/custom-call.0 | solution.py:17
  376.7 17.2 %all-reduce.15.cloned.1.call-done = f32[256,128]{0,1:T(8,128)} async-done(((f32[256,128]{0,1:T(8,128)}), f32[256,128]{0,1:T(8,128)}) %all-reduce.15.cloned.1.call-update) | async-done | bytes 131088 | tf_op jit(solution)/shard_map/psum | solution.py:11
  393.9 42.6 %all-gather.7.cloned.1.call-done = f32[2048,128]{0,1:T(8,128)} async-done(((f32[256,128]{0,1:T(8,128)}), f32[2048,128]{0,1:T(8,128)}) %all-gather.7.cloned.1.call-update) | async-done | bytes 1048592 | tf_op jit(solution)/shard_map/all_gather | solution.py:53
  436.6 2.1 reshape.89
  438.7 1.6 dynamic-slice_reduce_fusion
  445.0 17.9 %reduce-scatter.2.cloned.1.call-done = f32[256,2,256]{2,0,1:T(8,128)} async-done(((f32[256,4,256]{2,0,1:T(8,128)}), f32[256,2,256]{2,0,1:T(8,128)}) %reduce-scatter.2.cloned.1.call-update) | async-done | bytes 524304 | tf_op jit(solution)/shard_map/reduce_scatter | solution.py:73
  (109 shorter events, 30.6 us)
Async XLA Ops:
  6.5 77.9 %all-reduce.7.cloned.1.call-start = ((), (), s32[]{:S(2)}) async-start(), calls=%async_computation.1 | async-start | bytes 524288 | tf_op jit(solution)/shard_map/psum | solution.py:11
  9.6 156.2 %all-reduce.9.cloned.1.call-start = ((), (), s32[]{:S(2)}) async-start(), calls=%async_computation.2 | async-start | bytes 262144 | tf_op jit(solution)/shard_map/psum | solution.py:11
  84.4 1.2 copy-start.1
  148.5 60.0 %all-gather.5.cloned.1.call-start = ((), (), s32[]{:S(2)}) async-start(), calls=%async_computation.7 | async-start | bytes 1179648 | tf_op jit(solution)/shard_map/all_gather | solution.py:53
  165.8 71.7 %all-reduce.11.cloned.1.call-start = ((), (), s32[]{:S(2)}) async-start(), calls=%async_computation.3 | async-start | bytes 524288 | tf_op jit(solution)/shard_map/psum | solution.py:68
  212.2 0.9 copy-start.4
  215.0 96.7 %all-reduce.13.cloned.1.call-start = ((), (), s32[]{:S(2)}) async-start(), calls=%async_computation.4 | async-start | bytes 524288 | tf_op jit(solution)/shard_map/psum | solution.py:11
  239.2 154.7 %all-reduce.15.cloned.1.call-start = ((), (), s32[]{:S(2)}) async-start(), calls=%async_computation.5 | async-start | bytes 262144 | tf_op jit(solution)/shard_map/psum | solution.py:11
  311.8 1.2 copy-start.2
  374.6 1.0 copy-start.3
  376.6 59.9 %all-gather.7.cloned.1.call-start = ((), (), s32[]{:S(2)}) async-start(), calls=%async_computation.8 | async-start | bytes 1179648 | tf_op jit(solution)/shard_map/all_gather | solution.py:53
  393.9 69.0 %reduce-scatter.2.cloned.1.call-start = ((), (), s32[]{:S(2)}) async-start(), calls=%async_computation.6 | async-start | bytes 1572864 | tf_op jit(solution)/shard_map/reduce_scatter | solution.py:73
  440.3 0.9 copy-start.5
  443.3 1.2 copy-start
Sparse Core Ops, SparseCore 0:
  10.7 73.7 all-reduce.6
  148.7 17.0 all-reduce.8
  167.8 40.5 all-gather.4
  215.2 22.2 all-reduce.10
  240.7 71.0 all-reduce.12
  376.7 17.0 all-reduce.14
  395.9 40.5 all-gather.6
  443.5 19.3 reduce-scatter.1
where the time goes:
time: 481 us; the launch traced here: 472 us
  waiting for transfers between devices  307 us (64%)
  other arithmetic  113 us (23%)
  local copies, waits for them, and re-layouts  28.5 us (6%)
  between operations  16.8 us (3%)
  matrix products  5.65 us (1%)
    psum x4, waiting for transfers between devices, from_root(): return lax.psum(jnp.where(mine, shard, jnp.zeros_like(shard)), axis)  181 us
    all_gather x2, waiting for transfers between devices, on_device(): lax.all_gather(share.reshape(row_blocks, 1, block_size, half), 'row', axi...  85.2 us
    another operation x13, other arithmetic, factor_block(): lower_fac = jnp.linalg.cholesky(diag_block)  68.7 us
    another operation x5, other arithmetic, factor_block(): lax.linalg.triangular_solve(lower_fac, identity, left_side=True, lower=True)  39.4 us
    psum x1, waiting for transfers between devices, on_device(): head = lax.psum(update[:, :block_size], 'layer')  22.4 us
    reduce_scatter x1, waiting for transfers between devices, on_device(): lax.psum_scatter(total.reshape(rows, col_blocks, block_size), 'layer', sc...  17.9 us
  transfers between devices with their start and end apart: 8, of which 8 were waited for; matrix products, arithmetic and copies ran while one was open for 0% of the time, Pallas kernels for 0%

commit v1 on v0

--- a/solution.py
+++ b/solution.py
@@ -4,6 +4,28 @@
 from jax.sharding import PartitionSpec as P
 
 HIGH = lax.Precision.HIGHEST
+
+
+def laid_out(tiles, dim):
+    shape = list(tiles.shape[1:])
+    shape[dim] *= tiles.shape[0]
+    return jnp.moveaxis(tiles, 0, dim).reshape(shape)
+
+
+def doubled(x, axis):
+    length = lax.axis_size(axis)
+    blocks = x[None]
+    for level in range(length.bit_length() - 1):
+        bit = 1 << level
+        theirs = lax.ppermute(blocks, axis, [(i, i ^ bit) for i in range(length)])
+        both = jnp.stack([blocks, theirs])
+        upper = lax.axis_index(axis) >> level & 1
+        blocks = jnp.where(upper == 0, both, both[::-1]).reshape(-1, *x.shape)
+    return blocks
+
+
+def gather_by_bits(x, axis, dim):
+    return laid_out(doubled(x, axis), dim)
 
 
 def from_root(shard, axis, root):
@@ -50,9 +72,7 @@
         panels.append(complete)
         share = lax.dynamic_slice_in_dim(complete, grid_layer * half, half, 1)
         share = from_root(share, "col", section % col_total)
-        gathered = lax.all_gather(
-            share.reshape(row_blocks, 1, block_size, half), "row", axis=1, tiled=True
-        )
+        gathered = gather_by_bits(share.reshape(row_blocks, 1, block_size, half), "row", 1)
         grouped = gathered.reshape(col_blocks, col_total, block_size, half)
         picked = lax.dynamic_index_in_dim(grouped, grid_col, 1, keepdims=False).reshape(
             col_blocks * block_size, half

time: 481 us -> 465 us (0.967); the launches traced: 472 us -> 464 us
  waiting for transfers between devices: 307 us -> 290 us
  starting transfers between devices: 0.46 us -> 12.8 us
  local copies, waits for them, and re-layouts: 28.5 us -> 21.6 us
    all_gather x2 -> x0, waiting for transfers between devices: 85.2 us -> none  [on_device(): lax.all_gather(share.reshape(row_blocks, 1, block_size, half), 'row', axi...]
    ppermute x0 -> x6, waiting for transfers between devices: none -> 63.6 us  [doubled(): theirs = lax.ppermute(blocks, axis, [(i, i ^ bit) for i in range(length)])]
    ppermute x0 -> x6, starting transfers between devices: none -> 12.6 us  [doubled(): theirs = lax.ppermute(blocks, axis, [(i, i ^ bit) for i in range(length)])]
  transfers between devices with their start and end apart: 8 -> 12, of which waited for: 8 -> 12; matrix products, arithmetic and copies ran while one was open for 0% -> 0% of each run, Pallas kernels for 0% -> 0%
where the time goes in v1:
time: 465 us; the launch traced here: 464 us
  waiting for transfers between devices  290 us (62%)
  other arithmetic  117 us (25%)
  local copies, waits for them, and re-layouts  21.6 us (5%)
  between operations  16.5 us (4%)
  starting transfers between devices  12.8 us (3%)
  matrix products  5.66 us (1%)
    psum x4, waiting for transfers between devices, from_root(): return lax.psum(jnp.where(mine, shard, jnp.zeros_like(shard)), axis)  182 us
    another operation x13, other arithmetic, factor_block(): lower_fac = jnp.linalg.cholesky(diag_block)  68.6 us
    ppermute x6, waiting for transfers between devices, doubled(): theirs = lax.ppermute(blocks, axis, [(i, i ^ bit) for i in range(length)])  63.6 us
    another operation x5, other arithmetic, factor_block(): lax.linalg.triangular_solve(lower_fac, identity, left_side=True, lower=True)  39.4 us
    psum x1, waiting for transfers between devices, on_device(): head = lax.psum(update[:, :block_size], 'layer')  24.5 us
    reduce_scatter x1, waiting for transfers between devices, on_device(): lax.psum_scatter(total.reshape(rows, col_blocks, block_size), 'layer', sc...  19.9 us
    ppermute x6, starting transfers between devices, doubled(): theirs = lax.ppermute(blocks, axis, [(i, i ^ bit) for i in range(length)])  12.6 us
  transfers between devices with their start and end apart: 12, of which 12 were waited for; matrix products, arithmetic and copies ran while one was open for 0% of the time, Pallas kernels for 0%

profile of v1, /device:TPU:0, one launch (start us, length us, event | category | flops | bytes accessed | tf_op | source)
XLA Modules:
  0.0 464.4 jit_solution(6509699208277848412)
XLA Ops:
  9.8 74.7 %all-reduce.7.cloned.1.call-done = f32[256,256]{0,1:T(8,128)} async-done(((f32[256,256]{0,1:T(8,128)}), f32[256,256]{0,1:T(8,128)}) %all-reduce.7.cloned.1.call-update) | async-done | bytes 262160 | tf_op jit(solution)/shard_map/psum | solution.py:33
  85.7 11.7 %cholesky.130 = f32[128,128]{1,0:T(8,128)S(1)} custom-call(f32[128,128]{1,0:T(8,128)S(1)} %cholesky.194), custom_call_target="Cholesky" | custom-call | tf_op jit(solution)/shard_map/jit(cholesky)/cholesky | solution.py:37
  97.4 9.8 %custom-call.13 = f32[1,128,128]{1,2,0:T(8,128)S(1)} custom-call(f32[1,128,128]{2,1,0:T(8,128)S(1)} %get-tuple-element.82), custom_call_target="InvertDiagBlocksLowerTriangular" | custom-call | tf_op jit(solution)/shard_map/jit(cholesky)/cholesky | solution.py:37
  107.7 11.7 %cholesky.147 = f32[128,128]{1,0:T(8,128)S(1)} custom-call(f32[128,128]{1,0:T(8,128)S(1)} %convolution_subtract_fusion.3), custom_call_target="Cholesky" | custom-call | tf_op jit(solution)/shard_map/jit(cholesky)/cholesky | solution.py:37
  121.8 4.2 while.4
  126.0 19.7 %custom-call.14 = f32[2,128,128]{1,2,0:T(8,128)S(1)} custom-call(f32[2,128,128]{2,1,0:T(8,128)S(1)} %get-tuple-element.21), custom_call_target="InvertDiagBlocksLowerTriangular" | custom-call | tf_op jit(solution)/shard_map/triangular_solve/custom-call.0 | solution.py:39
  147.8 17.2 %all-reduce.9.cloned.1.call-done = f32[256,128]{0,1:T(8,128)} async-done(((f32[256,128]{0,1:T(8,128)}), f32[256,128]{0,1:T(8,128)}) %all-reduce.9.cloned.1.call-update) | async-done | bytes 131088 | tf_op jit(solution)/shard_map/psum | solution.py:33
  166.8 4.1 collective-permute-done
  173.7 5.9 %collective-permute-done.1 = f32[2,1,1,256,128]{3,4,0,2,1:T(8,128)S(1)} collective-permute-done((f32[2,1,1,256,128]{3,4,0,2,1:T(8,128)S(1)}, f32[2,1,1,256,128]{3,4,0,2,1:T(8,128)S(1)}, u32[]{:S(2)}, u32[]{:S(2)}) %collective-permute-start.1) | collective-permute-done | bytes 262176 | tf_op jit(solution)/shard_map/ppermute | solution.py:20
  179.9 2.7 collective-permute-start.2
  182.8 21.8 %collective-permute-done.2 = f32[4,1,1,256,128]{4,3,0,2,1:T(8,128)} collective-permute-done((f32[4,1,1,256,128]{4,3,0,2,1:T(8,128)S(1)}, f32[4,1,1,256,128]{4,3,0,2,1:T(8,128)}, u32[]{:S(2)}, u32[]{:S(2)}) %collective-permute-start.2) | collective-permute-done | bytes 524320 | tf_op jit(solution)/shard_map/ppermute | solution.py:20
  208.7 24.5 %all-reduce.11.cloned.1.call-done = f32[256,256]{0,1:T(8,128)} async-done(((f32[256,256]{0,1:T(8,128)}), f32[256,256]{0,1:T(8,128)}) %all-reduce.11.cloned.1.call-update) | async-done | bytes 262160 | tf_op jit(solution)/shard_map/psum | solution.py:88
  235.0 72.5 %all-reduce.13.cloned.1.call-done = f32[256,256]{0,1:T(8,128)} async-done(((f32[256,256]{0,1:T(8,128)}), f32[256,256]{0,1:T(8,128)}) %all-reduce.13.cloned.1.call-update) | async-done | bytes 262160 | tf_op jit(solution)/shard_map/psum | solution.py:33
  308.7 11.7 %cholesky.164 = f32[128,128]{1,0:T(8,128)S(1)} custom-call(f32[128,128]{1,0:T(8,128)S(1)} %cholesky.197), custom_call_target="Cholesky" | custom-call | tf_op jit(solution)/shard_map/jit(cholesky)/cholesky | solution.py:37
  320.4 9.8 %custom-call.15 = f32[1,128,128]{1,2,0:T(8,128)S(1)} custom-call(f32[1,128,128]{2,1,0:T(8,128)S(1)} %get-tuple-element.80), custom_call_target="InvertDiagBlocksLowerTriangular" | custom-call | tf_op jit(solution)/shard_map/jit(cholesky)/cholesky | solution.py:37
  330.7 11.7 %cholesky.181 = f32[128,128]{1,0:T(8,128)S(1)} custom-call(f32[128,128]{1,0:T(8,128)S(1)} %convolution_subtract_fusion.2), custom_call_target="Cholesky" | custom-call | tf_op jit(solution)/shard_map/jit(cholesky)/cholesky | solution.py:37
  345.5 4.4 while.5
  349.9 19.7 %custom-call.16 = f32[2,128,128]{1,2,0:T(8,128)S(1)} custom-call(f32[2,128,128]{2,1,0:T(8,128)S(1)} %get-tuple-element.22), custom_call_target="InvertDiagBlocksLowerTriangular" | custom-call | tf_op jit(solution)/shard_map/triangular_solve/custom-call.0 | solution.py:39
  372.4 17.2 %all-reduce.15.cloned.1.call-done = f32[256,128]{0,1:T(8,128)} async-done(((f32[256,128]{0,1:T(8,128)}), f32[256,128]{0,1:T(8,128)}) %all-reduce.15.cloned.1.call-update) | async-done | bytes 131088 | tf_op jit(solution)/shard_map/psum | solution.py:33
  391.3 4.1 collective-permute-done.3
  398.3 5.9 %collective-permute-done.4 = f32[2,1,1,256,128]{3,4,0,2,1:T(8,128)S(1)} collective-permute-done((f32[2,1,1,256,128]{3,4,0,2,1:T(8,128)S(1)}, f32[2,1,1,256,128]{3,4,0,2,1:T(8,128)S(1)}, u32[]{:S(2)}, u32[]{:S(2)}) %collective-permute-start.4) | collective-permute-done | bytes 262176 | tf_op jit(solution)/shard_map/ppermute | solution.py:20
  404.4 2.7 collective-permute-start.5
  407.3 21.8 %collective-permute-done.5 = f32[4,1,1,256,128]{4,3,0,2,1:T(8,128)} collective-permute-done((f32[4,1,1,256,128]{4,3,0,2,1:T(8,128)S(1)}, f32[4,1,1,256,128]{4,3,0,2,1:T(8,128)}, u32[]{:S(2)}, u32[]{:S(2)}) %collective-permute-start.5) | collective-permute-done | bytes 524320 | tf_op jit(solution)/shard_map/ppermute | solution.py:20
  435.1 19.9 %reduce-scatter.2.cloned.1.call-done = f32[256,2,256]{2,0,1:T(8,128)} async-done(((f32[256,4,256]{2,0,1:T(8,128)}), f32[256,2,256]{2,0,1:T(8,128)}) %reduce-scatter.2.cloned.1.call-update) | async-done | bytes 524304 | tf_op jit(solution)/shard_map/reduce_scatter | solution.py:93
  (127 shorter events, 46.4 us)
Async XLA Ops:
  6.5 77.9 %all-reduce.7.cloned.1.call-start = ((), (), s32[]{:S(2)}) async-start(), calls=%async_computation.1 | async-start | bytes 524288 | tf_op jit(solution)/shard_map/psum | solution.py:33
  9.6 155.4 %all-reduce.9.cloned.1.call-start = ((), (), s32[]{:S(2)}) async-start(), calls=%async_computation.2 | async-start | bytes 262144 | tf_op jit(solution)/shard_map/psum | solution.py:33
  84.4 1.2 copy-start.1
  147.8 85.4 %all-reduce.11.cloned.1.call-start = ((), (), s32[]{:S(2)}) async-start(), calls=%async_computation.3 | async-start | bytes 524288 | tf_op jit(solution)/shard_map/psum | solution.py:88
  165.0 5.9 %collective-permute-start = (f32[1,1,1,256,128]{3,4,2,1,0:T(8,128)}, f32[1,1,1,256,128]{3,4,2,1,0:T(8,128)S(1)}, u32[]{:S(2)}, u32[]{:S(2)}) collective-permute-start(f32[1,1,1,256,128]{3,4,2,1,0:T(8,128)} %bitcast.127), channel_id=1, source_target_pairs={{0,4},{4,0},{8,12},{12,8},{16,20},{20,16},{24,28},{28,24},{1,5},{5... | collective-permute-start | bytes 393224 | tf_op jit(solution)/shard_map/ppermute | solution.py:20
  171.9 7.7 %collective-permute-start.1 = (f32[2,1,1,256,128]{3,4,0,2,1:T(8,128)S(1)}, f32[2,1,1,256,128]{3,4,0,2,1:T(8,128)S(1)}, u32[]{:S(2)}, u32[]{:S(2)}) collective-permute-start(f32[2,1,1,256,128]{3,4,0,2,1:T(8,128)S(1)} %get-tuple-element.78), channel_id=1, source_target_pairs={{0,8},{4,12},{8,0},{12,4},{16,24},{20,28},{24,16},{28,20},{1,9},{5... | collective-permute-start | bytes 786440 | tf_op jit(solution)/shard_map/ppermute | solution.py:20
  179.9 24.7 %collective-permute-start.2 = (f32[4,1,1,256,128]{4,3,0,2,1:T(8,128)S(1)}, f32[4,1,1,256,128]{4,3,0,2,1:T(8,128)}, u32[]{:S(2)}, u32[]{:S(2)}) collective-permute-start(f32[4,1,1,256,128]{4,3,0,2,1:T(8,128)S(1)} %copy.61), channel_id=1, source_target_pairs={{0,16},{4,20},{8,24},{12,28},{16,0},{20,4},{24,8},{28,12},{1,17},{... | collective-permute-start | bytes 1572872 | tf_op jit(solution)/shard_map/ppermute | solution.py:20
  205.8 0.9 copy-start.4
  208.6 98.8 %all-reduce.13.cloned.1.call-start = ((), (), s32[]{:S(2)}) async-start(), calls=%async_computation.4 | async-start | bytes 524288 | tf_op jit(solution)/shard_map/psum | solution.py:33
  234.9 154.7 %all-reduce.15.cloned.1.call-start = ((), (), s32[]{:S(2)}) async-start(), calls=%async_computation.5 | async-start | bytes 262144 | tf_op jit(solution)/shard_map/psum | solution.py:33
  307.5 1.2 copy-start.2
  370.2 1.0 copy-start.3
  372.3 82.7 %reduce-scatter.2.cloned.1.call-start = ((), (), s32[]{:S(2)}) async-start(), calls=%async_computation.6 | async-start | bytes 1572864 | tf_op jit(solution)/shard_map/reduce_scatter | solution.py:93
  389.6 5.9 %collective-permute-start.3 = (f32[1,1,1,256,128]{3,4,2,1,0:T(8,128)}, f32[1,1,1,256,128]{3,4,2,1,0:T(8,128)S(1)}, u32[]{:S(2)}, u32[]{:S(2)}) collective-permute-start(f32[1,1,1,256,128]{3,4,2,1,0:T(8,128)} %bitcast.129), channel_id=1, source_target_pairs={{0,4},{4,0},{8,12},{12,8},{16,20},{20,16},{24,28},{28,24},{1,5},{5... | collective-permute-start | bytes 393224 | tf_op jit(solution)/shard_map/ppermute | solution.py:20
  396.4 7.7 %collective-permute-start.4 = (f32[2,1,1,256,128]{3,4,0,2,1:T(8,128)S(1)}, f32[2,1,1,256,128]{3,4,0,2,1:T(8,128)S(1)}, u32[]{:S(2)}, u32[]{:S(2)}) collective-permute-start(f32[2,1,1,256,128]{3,4,0,2,1:T(8,128)S(1)} %get-tuple-element.76), channel_id=1, source_target_pairs={{0,8},{4,12},{8,0},{12,4},{16,24},{20,28},{24,16},{28,20},{1,9},{5... | collective-permute-start | bytes 786440 | tf_op jit(solution)/shard_map/ppermute | solution.py:20
  404.4 24.7 %collective-permute-start.5 = (f32[4,1,1,256,128]{4,3,0,2,1:T(8,128)S(1)}, f32[4,1,1,256,128]{4,3,0,2,1:T(8,128)}, u32[]{:S(2)}, u32[]{:S(2)}) collective-permute-start(f32[4,1,1,256,128]{4,3,0,2,1:T(8,128)S(1)} %copy.73), channel_id=1, source_target_pairs={{0,16},{4,20},{8,24},{12,28},{16,0},{20,4},{24,8},{28,12},{1,17},{... | collective-permute-start | bytes 1572872 | tf_op jit(solution)/shard_map/ppermute | solution.py:20
  430.3 0.9 copy-start.5
  433.4 1.2 copy-start
Sparse Core Ops, SparseCore 0:
  10.7 73.7 all-reduce.6
  147.9 17.0 all-reduce.8
  208.8 24.3 all-reduce.10
  236.4 71.0 all-reduce.12
  372.4 17.0 all-reduce.14
  433.5 21.4 reduce-scatter.1
